TPU v7x, 256 devices: a whole 4x4x8 slice. The times are simulated.
256 devices in a mesh: illum: 16 (over z_hi, x), row: 4 (over y), col: 4 (over z_lo, core).
Axes of the slice: x: 4, y: 4, z: 8 (z_hi: 4, z_lo: 2; z = z_hi * 2 + z_lo), core: 2. Of those that a mesh axis runs over, the one named last changes fastest.
Arguments:
- phase_delay: float32 [2, 512, 4096], P(None, ('row', 'illum'), 'col'), may hold values from -1 to 1
- angles: int32 [16, 2], P('illum'), may hold values from -8 to 8
- measured: bfloat16 [2, 16, 512, 4096], P(None, 'illum', 'row', 'col'), may hold values from -120 to 120, as said below
Outputs:
- phase_grad: float32 [2, 512, 4096], P(None, ('row', 'illum'), 'col')
Inputs may be any that keep to these rules, and one draw needn't show every extreme that they name: Real and imaginary parts of a measured field, with scales that vary over rows and columns.
All inputs are finite; a program needn't handle non-finite values.
Results may differ from a plain program's by a relative error of at most 0.0003.
Values sent between devices are 32-bit elements; how exact they have to be, the bound alone decides.
A program may use at most 64 MiB of HBM per device.

v0:
```python
import math
import jax
import jax.numpy as jnp
from jax import lax
from jax.sharding import PartitionSpec as P

SWEEPS = 2
beta_step = 0.5
eps_energy = 1e-06


def with_halo(x, sides, width):
    for axis, dim in sides:
        peers, length = (lax.axis_size(axis), x.shape[dim])
        up = [(i, (i + 1) % peers) for i in range(peers - 1)]
        down = [(j, i) for i, j in up]
        last = lax.slice_in_dim(x, length - width, length, axis=dim)
        first = lax.slice_in_dim(x, 0, width, axis=dim)
        before = lax.ppermute(last, axis, up)
        after = lax.ppermute(first, axis, down)
        x = jnp.concatenate([before, x, after], axis=dim)
    return x


def neighbour_sum(padded):
    return (
        padded[..., 2:, 1:-1]
        + padded[..., :-2, 1:-1]
        + padded[..., 1:-1, 2:]
        + padded[..., 1:-1, :-2]
    )


def exchange_rims(wave_field):
    return with_halo(wave_field, (("row", 2), ("col", 3)), 1)


def propagate(wave_field, direction):
    beta_sign = direction * beta_step
    divisor = 1.0 + 16.0 * beta_sign * beta_sign
    beside_all = neighbour_sum(exchange_rims(wave_field))
    real_part, imag_part = (wave_field[0], wave_field[1])
    rhs_real = real_part + 4.0 * beta_sign * imag_part - beta_sign * beside_all[1]
    rhs_imag = imag_part - 4.0 * beta_sign * real_part + beta_sign * beside_all[0]
    for sweep in range(SWEEPS):
        if sweep > 0:
            beside_all = neighbour_sum(exchange_rims(jnp.stack([real_part, imag_part])))
        total_real = rhs_real - beta_sign * beside_all[1]
        total_imag = rhs_imag + beta_sign * beside_all[0]
        real_part = (total_real + 4.0 * beta_sign * total_imag) / divisor
        imag_part = (total_imag - 4.0 * beta_sign * total_real) / divisor
    return jnp.stack([real_part, imag_part])


def per_device(phase_delay, angles, measured):
    illum_count = lax.axis_size("illum")
    stripe = phase_delay.shape[1]
    rows_tile = stripe * illum_count
    cols_tile = measured.shape[3]
    total_rows = rows_tile * lax.axis_size("row")
    total_cols = cols_tile * lax.axis_size("col")
    row_ids = lax.axis_index("row") * rows_tile + lax.iota(jnp.int32, rows_tile)
    col_ids = lax.axis_index("col") * cols_tile + lax.iota(jnp.int32, cols_tile)

    def advance(field_now, direction):
        return propagate(field_now, direction)

    along_x = angles[:, 0:1] * row_ids[None, :] % total_rows
    along_y = angles[:, 1:2] * col_ids[None, :] % total_cols
    angle_phase = (
        2.0
        * math.pi
        * (
            along_x.astype(jnp.float32)[:, :, None] / total_rows
            + along_y.astype(jnp.float32)[:, None, :] / total_cols
        )
    )
    wave_field = jnp.stack([jnp.cos(angle_phase), jnp.sin(angle_phase)])
    target = measured.astype(jnp.float32)
    energy = (
        lax.psum(jnp.sum(target * target, axis=(0, 2, 3)), ("row", "col"))
        / (total_rows * total_cols)
        + eps_energy
    )
    all_planes = lax.all_gather(phase_delay, "illum", axis=1, tiled=True)
    stored = []
    for depth_index in range(phase_delay.shape[0]):
        phase_plane = all_planes[depth_index]
        cosine = jnp.cos(phase_plane)
        sine_part = jnp.sin(phase_plane)
        modulated = jnp.stack(
            [
                wave_field[0] * cosine - wave_field[1] * sine_part,
                wave_field[0] * sine_part + wave_field[1] * cosine,
            ]
        )
        stored.append((modulated, cosine, sine_part))
        wave_field = advance(modulated, 1.0)
    adjoint_wave = 2.0 * (wave_field - target) / energy[None, :, None, None]
    slice_grads = [None] * len(stored)
    for depth_index in reversed(range(len(stored))):
        modulated, cosine, sine_part = stored[depth_index]
        adjoint_wave = advance(adjoint_wave, -1.0)
        slice_grads[depth_index] = jnp.sum(
            adjoint_wave[1] * modulated[0] - adjoint_wave[0] * modulated[1], axis=0
        )
        if depth_index > 0:
            adjoint_wave = jnp.stack(
                [
                    adjoint_wave[0] * cosine + adjoint_wave[1] * sine_part,
                    adjoint_wave[1] * cosine - adjoint_wave[0] * sine_part,
                ]
            )
    local_grads = jnp.stack(slice_grads)
    summed = lax.psum(local_grads, "illum")
    return lax.dynamic_slice_in_dim(summed, lax.axis_index("illum") * stripe, stripe, 1)


def solution(mesh):
    placed = (P(None, ("row", "illum"), "col"), P("illum", None), P(None, "illum", "row", "col"))
    return jax.shard_map(
        per_device,
        mesh=mesh,
        in_specs=placed,
        out_specs=P(None, ("row", "illum"), "col"),
        check_vma=False,
    )
```

profile of v0, /device:TPU:2, one launch (start us, length us, event | category | flops | bytes accessed | tf_op | source)
XLA Modules:
  0.0 428.9 jit_solution(10566999443613107633)
XLA Ops:
  9.8 55.3 %all-gather.2.cloned.1.call-done = f32[2,128,1024]{2,1,0:T(8,128)} async-done(((f32[2,8,1024]{2,1,0:T(8,128)}), f32[2,128,1024]{2,1,0:T(8,128)}) %all-gather.2.cloned.1.call-update) | async-done | bytes 1048592 | tf_op jit(solution)/shard_map/all_gather | solution.py:85
  65.1 4.8 %fusion.64 = (f32[1,1,128,1024]{3,2,1,0:T(8,128)S(1)}, f32[1,1,128,1024]{3,2,1,0:T(8,128)S(1)}) fusion(f32[2,128,1024]{2,1,0:T(8,128)} %all-gather.2.cloned.1.call-done, f32[1024]{0:T(1024)S(1)} %fusion.60, f32[128]{0:T(128)S(1)} %fusion.62), kind=kLoop, calls=%fused_computation.267 | loop fusion | flops 1048576 | bytes 1577472 | tf_op jit(solution)/shard_map/stack | solution.py:91
  70.0 3.4 collective-permute-start.1
  73.4 1.3 collective-permute-start
  74.7 4.2 collective-permute-done
  79.0 1.3 collective-permute-start.2
  80.3 3.2 collective-permute-start.3
  85.2 4.2 multiply_bitcast_fusion.7
  89.4 3.4 collective-permute-start.5
  92.8 1.3 collective-permute-start.4
  94.2 4.2 collective-permute-done.4
  98.5 1.3 collective-permute-start.6
  99.8 3.0 collective-permute-start.7
  104.5 6.1 %multiply_subtract_fusion.3 = (f32[1,128,1024]{2,1,0:T(8,128)S(1)}, f32[1,128,1024]{2,1,0:T(8,128)S(1)}) fusion(f32[2,128,1024]{2,1,0:T(8,128)S(1)} %copy-done, f32[2,1,128,1024]{3,2,1,0:T(8,128)S(1)} %fusion.21, f32[2,1,128,1024]{3,2,1,0:T(8,128)S(1)} %fusion.24, f32[1024]{0:T(1024)S(1)} %fusion.60, f32[128]{0:T(128)S(1)} %fusion.62), kind=kLoop, calls=%fused_computation.187 | loop fusion | flops 4194304 | bytes 4198912 | tf_op jit(solution)/shard_map/sub | solution.py:93
  110.6 3.1 collective-permute-start.9
  113.7 1.3 collective-permute-start.8
  115.1 4.2 collective-permute-done.8
  119.4 1.3 collective-permute-start.10
  120.7 5.5 %collective-permute-start.11 = (f32[2,1,130,1]{3,2,1,0:T(8,128)S(1)}, f32[2,1,130,1]{3,2,1,0:T(8,128)S(1)}, u32[]{:S(2)}, u32[]{:S(2)}) collective-permute-start(f32[2,1,130,1]{3,2,1,0:T(8,128)S(1)} %get-tuple-element.33), channel_id=1, source_target_pairs={{0,1},{1,2},{2,3},{4,5},{5,6},{6,7},{8,9},{9,10},{10,11},{12,13},{... | collective-permute-start | bytes 3128 | tf_op jit(solution)/shard_map/ppermute | solution.py:19
  129.1 2.2 collective-permute-start.13
  131.3 1.4 collective-permute-start.12
  132.8 4.2 collective-permute-done.12
  139.1 5.7 %collective-permute-start.15 = (f32[2,1,130,1]{3,2,1,0:T(8,128)}, f32[2,1,130,1]{3,2,1,0:T(8,128)S(1)}, u32[]{:S(2)}, u32[]{:S(2)}) collective-permute-start(f32[2,1,130,1]{3,2,1,0:T(8,128)} %get-tuple-element.31), channel_id=1, source_target_pairs={{0,1},{1,2},{2,3},{4,5},{5,6},{6,7},{8,9},{9,10},{10,11},{12,13},{... | collective-permute-start | bytes 3128 | tf_op jit(solution)/shard_map/ppermute | solution.py:19
  145.7 31.6 %psum.14 = f32[1]{0:T(128)} all-reduce(f32[1]{0:T(128)} %bitcast.20), channel_id=1, replica_groups=mesh['illum'=16,'row'=4,'col'=4] {'row','col'}, use_global_device_ids=true, to_apply=%region_1.2 | all-reduce | flops 1 | bytes 8 | tf_op jit(solution)/shard_map/psum | solution.py:81
  181.8 1.3 collective-permute-start.16
  183.1 4.2 collective-permute-done.16
  187.4 1.3 collective-permute-start.18
  188.7 3.0 collective-permute-start.19
  193.8 1.6 collective-permute-start.21
  195.4 1.3 collective-permute-start.20
  196.8 4.2 collective-permute-done.20
  201.1 1.3 collective-permute-start.22
  202.4 3.2 collective-permute-start.23
  207.1 2.3 multiply_add_fusion
  209.4 2.1 multiply_subtract_fusion.2
  211.5 1.9 collective-permute-start.25
  213.5 1.3 collective-permute-start.24
  214.8 4.2 collective-permute-done.24
  219.1 1.3 collective-permute-start.26
  220.4 5.2 %collective-permute-start.27 = (f32[2,1,130,1]{3,2,1,0:T(8,128)S(1)}, f32[2,1,130,1]{3,2,1,0:T(8,128)S(1)}, u32[]{:S(2)}, u32[]{:S(2)}) collective-permute-start(f32[2,1,130,1]{3,2,1,0:T(8,128)S(1)} %get-tuple-element.25), channel_id=1, source_target_pairs={{0,1},{1,2},{2,3},{4,5},{5,6},{6,7},{8,9},{9,10},{10,11},{12,13},{... | collective-permute-start | bytes 3128 | tf_op jit(solution)/shard_map/ppermute | solution.py:19
  227.9 2.2 collective-permute-start.29
  230.1 1.3 collective-permute-start.28
  231.5 4.2 collective-permute-done.28
  235.8 1.3 collective-permute-start.30
  237.1 5.7 %collective-permute-start.31 = (f32[2,1,130,1]{3,2,1,0:T(8,128)S(1)}, f32[2,1,130,1]{3,2,1,0:T(8,128)S(1)}, u32[]{:S(2)}, u32[]{:S(2)}) collective-permute-start(f32[2,1,130,1]{3,2,1,0:T(8,128)S(1)} %get-tuple-element.23), channel_id=1, source_target_pairs={{0,1},{1,2},{2,3},{4,5},{5,6},{6,7},{8,9},{9,10},{10,11},{12,13},{... | collective-permute-start | bytes 3128 | tf_op jit(solution)/shard_map/ppermute | solution.py:19
  244.5 4.1 multiply_subtract_fusion.1
  249.7 170.8 %all-reduce.2.cloned.1.call-done = f32[2,128,1024]{2,1,0:T(8,128)} async-done(((f32[2,128,1024]{2,1,0:T(8,128)}), f32[2,128,1024]{2,1,0:T(8,128)}) %all-reduce.2.cloned.1.call-update) | async-done | bytes 1048592 | tf_op jit(solution)/shard_map/psum | solution.py:115
  420.5 1.5 constant_dynamic-slice_fusion
  (82 shorter events, 25.6 us)
Async XLA Ops:
  6.5 58.6 %all-gather.2.cloned.1.call-start = ((), (), s32[]{:S(2)}) async-start(), calls=%async_computation | async-start | bytes 1114112 | tf_op jit(solution)/shard_map/all_gather | solution.py:85
  7.3 413.3 %all-reduce.2.cloned.1.call-start = ((), (), s32[]{:S(2)}) async-start(), calls=%async_computation.1 | async-start | bytes 2097152 | tf_op jit(solution)/shard_map/psum | solution.py:115
  7.3 0.7 copy-start.7
  70.0 4.7 %collective-permute-start.1 = (f32[2,1,1,1024]{3,2,1,0:T(1,128)S(1)}, f32[2,1,1,1024]{3,2,1,0:T(1,128)S(1)}, u32[]{:S(2)}, u32[]{:S(2)}) collective-permute-start(f32[2,1,1,1024]{3,2,1,0:T(1,128)S(1)} %get-tuple-element.56), channel_id=1, source_target_pairs={{0,4},{4,8},{8,12},{1,5},{5,9},{9,13},{2,6},{6,10},{10,14},{3,7},{... | collective-permute-start | bytes 24584 | tf_op jit(solution)/shard_map/ppermute | solution.py:19
  73.4 5.5 %collective-permute-start = (f32[2,1,1,1024]{3,2,1,0:T(1,128)S(1)}, f32[2,1,1,1024]{3,2,1,0:T(1,128)S(1)}, u32[]{:S(2)}, u32[]{:S(2)}) collective-permute-start(f32[2,1,1,1024]{3,2,1,0:T(1,128)S(1)} %get-tuple-element.57), channel_id=1, source_target_pairs={{4,0},{8,4},{12,8},{5,1},{9,5},{13,9},{6,2},{10,6},{14,10},{7,3},{... | collective-permute-start | bytes 24584 | tf_op jit(solution)/shard_map/ppermute | solution.py:20
  79.0 4.5 %collective-permute-start.2 = (f32[2,1,130,1]{3,2,1,0:T(8,128)S(1)}, f32[2,1,130,1]{3,2,1,0:T(8,128)S(1)}, u32[]{:S(2)}, u32[]{:S(2)}) collective-permute-start(f32[2,1,130,1]{3,2,1,0:T(8,128)S(1)} %get-tuple-element.36), channel_id=1, source_target_pairs={{1,0},{2,1},{3,2},{5,4},{6,5},{7,6},{9,8},{10,9},{11,10},{13,12},{... | collective-permute-start | bytes 3128 | tf_op jit(solution)/shard_map/ppermute | solution.py:20
  80.3 4.8 %copy-start = (f32[2,128,1024]{2,1,0:T(8,128)S(1)}, f32[2,128,1024]{2,1,0:T(8,128)}, u32[]{:S(2)}) copy-start(f32[2,128,1024]{2,1,0:T(8,128)} %all-gather.2.cloned.1.call-done) | copy-start | bytes 3145732
  80.3 4.1 collective-permute-start.3
  89.4 4.8 %collective-permute-start.5 = (f32[2,1,1,1024]{3,2,1,0:T(1,128)S(1)}, f32[2,1,1,1024]{3,2,1,0:T(1,128)S(1)}, u32[]{:S(2)}, u32[]{:S(2)}) collective-permute-start(f32[2,1,1,1024]{3,2,1,0:T(1,128)S(1)} %get-tuple-element.54), channel_id=1, source_target_pairs={{0,4},{4,8},{8,12},{1,5},{5,9},{9,13},{2,6},{6,10},{10,14},{3,7},{... | collective-permute-start | bytes 24584 | tf_op jit(solution)/shard_map/ppermute | solution.py:19
  92.8 5.5 %collective-permute-start.4 = (f32[2,1,1,1024]{3,2,1,0:T(1,128)S(1)}, f32[2,1,1,1024]{3,2,1,0:T(1,128)S(1)}, u32[]{:S(2)}, u32[]{:S(2)}) collective-permute-start(f32[2,1,1,1024]{3,2,1,0:T(1,128)S(1)} %get-tuple-element.55), channel_id=1, source_target_pairs={{4,0},{8,4},{12,8},{5,1},{9,5},{13,9},{6,2},{10,6},{14,10},{7,3},{... | collective-permute-start | bytes 24584 | tf_op jit(solution)/shard_map/ppermute | solution.py:20
  98.5 4.3 %collective-permute-start.6 = (f32[2,1,130,1]{3,2,1,0:T(8,128)S(1)}, f32[2,1,130,1]{3,2,1,0:T(8,128)S(1)}, u32[]{:S(2)}, u32[]{:S(2)}) collective-permute-start(f32[2,1,130,1]{3,2,1,0:T(8,128)S(1)} %get-tuple-element.34), channel_id=1, source_target_pairs={{1,0},{2,1},{3,2},{5,4},{6,5},{7,6},{9,8},{10,9},{11,10},{13,12},{... | collective-permute-start | bytes 3128 | tf_op jit(solution)/shard_map/ppermute | solution.py:20
  99.8 4.0 collective-permute-start.7
  110.6 4.5 %collective-permute-start.9 = (f32[2,1,1,1024]{3,2,1,0:T(1,128)S(1)}, f32[2,1,1,1024]{3,2,1,0:T(1,128)S(1)}, u32[]{:S(2)}, u32[]{:S(2)}) collective-permute-start(f32[2,1,1,1024]{3,2,1,0:T(1,128)S(1)} %get-tuple-element.52), channel_id=1, source_target_pairs={{0,4},{4,8},{8,12},{1,5},{5,9},{9,13},{2,6},{6,10},{10,14},{3,7},{... | collective-permute-start | bytes 24584 | tf_op jit(solution)/shard_map/ppermute | solution.py:19
  113.7 5.5 %collective-permute-start.8 = (f32[2,1,1,1024]{3,2,1,0:T(1,128)S(1)}, f32[2,1,1,1024]{3,2,1,0:T(1,128)S(1)}, u32[]{:S(2)}, u32[]{:S(2)}) collective-permute-start(f32[2,1,1,1024]{3,2,1,0:T(1,128)S(1)} %get-tuple-element.53), channel_id=1, source_target_pairs={{4,0},{8,4},{12,8},{5,1},{9,5},{13,9},{6,2},{10,6},{14,10},{7,3},{... | collective-permute-start | bytes 24584 | tf_op jit(solution)/shard_map/ppermute | solution.py:20
  119.4 6.8 %collective-permute-start.10 = (f32[2,1,130,1]{3,2,1,0:T(8,128)S(1)}, f32[2,1,130,1]{3,2,1,0:T(8,128)S(1)}, u32[]{:S(2)}, u32[]{:S(2)}) collective-permute-start(f32[2,1,130,1]{3,2,1,0:T(8,128)S(1)} %get-tuple-element.32), channel_id=1, source_target_pairs={{1,0},{2,1},{3,2},{5,4},{6,5},{7,6},{9,8},{10,9},{11,10},{13,12},{... | collective-permute-start | bytes 3128 | tf_op jit(solution)/shard_map/ppermute | solution.py:20
  120.7 6.4 %collective-permute-start.11 = (f32[2,1,130,1]{3,2,1,0:T(8,128)S(1)}, f32[2,1,130,1]{3,2,1,0:T(8,128)S(1)}, u32[]{:S(2)}, u32[]{:S(2)}) collective-permute-start(f32[2,1,130,1]{3,2,1,0:T(8,128)S(1)} %get-tuple-element.33), channel_id=1, source_target_pairs={{0,1},{1,2},{2,3},{4,5},{5,6},{6,7},{8,9},{9,10},{10,11},{12,13},{... | collective-permute-start | bytes 3128 | tf_op jit(solution)/shard_map/ppermute | solution.py:19
  128.1 0.8 copy-start.1
  128.1 1.0 copy-start.3
  129.1 3.7 collective-permute-start.13
  131.3 13.5 %copy-start.5 = (bf16[2,1,128,1024]{3,2,1,0:T(8,128)(2,1)S(1)}, bf16[2,1,128,1024]{3,2,1,0:T(8,128)(2,1)}, u32[]{:S(2)}) copy-start(bf16[2,1,128,1024]{3,2,1,0:T(8,128)(2,1)} %param.5) | copy-start | bytes 1572868
  131.3 5.7 %collective-permute-start.12 = (f32[2,1,1,1024]{3,2,1,0:T(1,128)S(1)}, f32[2,1,1,1024]{3,2,1,0:T(1,128)S(1)}, u32[]{:S(2)}, u32[]{:S(2)}) collective-permute-start(f32[2,1,1,1024]{3,2,1,0:T(1,128)S(1)} %get-tuple-element.51), channel_id=1, source_target_pairs={{4,0},{8,4},{12,8},{5,1},{9,5},{13,9},{6,2},{10,6},{14,10},{7,3},{... | collective-permute-start | bytes 24584 | tf_op jit(solution)/shard_map/ppermute | solution.py:20
  137.8 40.2 %collective-permute-start.14 = (f32[2,1,130,1]{3,2,1,0:T(8,128)}, f32[2,1,130,1]{3,2,1,0:T(8,128)S(1)}, u32[]{:S(2)}, u32[]{:S(2)}) collective-permute-start(f32[2,1,130,1]{3,2,1,0:T(8,128)} %get-tuple-element.30), channel_id=1, source_target_pairs={{1,0},{2,1},{3,2},{5,4},{6,5},{7,6},{9,8},{10,9},{11,10},{13,12},{... | collective-permute-start | bytes 3128 | tf_op jit(solution)/shard_map/ppermute | solution.py:20
  139.1 38.9 %collective-permute-start.15 = (f32[2,1,130,1]{3,2,1,0:T(8,128)}, f32[2,1,130,1]{3,2,1,0:T(8,128)S(1)}, u32[]{:S(2)}, u32[]{:S(2)}) collective-permute-start(f32[2,1,130,1]{3,2,1,0:T(8,128)} %get-tuple-element.31), channel_id=1, source_target_pairs={{0,1},{1,2},{2,3},{4,5},{5,6},{6,7},{8,9},{9,10},{10,11},{12,13},{... | collective-permute-start | bytes 3128 | tf_op jit(solution)/shard_map/ppermute | solution.py:19
  178.0 1.0 copy-start.2
  178.0 1.2 copy-start.4
  179.2 1.0 copy-start.6
  180.5 2.6 collective-permute-start.17
  181.8 5.5 %collective-permute-start.16 = (f32[2,1,1,1024]{3,2,1,0:T(1,128)S(1)}, f32[2,1,1,1024]{3,2,1,0:T(1,128)S(1)}, u32[]{:S(2)}, u32[]{:S(2)}) collective-permute-start(f32[2,1,1,1024]{3,2,1,0:T(1,128)S(1)} %get-tuple-element.49), channel_id=1, source_target_pairs={{4,0},{8,4},{12,8},{5,1},{9,5},{13,9},{6,2},{10,6},{14,10},{7,3},{... | collective-permute-start | bytes 24584 | tf_op jit(solution)/shard_map/ppermute | solution.py:20
  187.4 4.3 %collective-permute-start.18 = (f32[2,1,130,1]{3,2,1,0:T(8,128)S(1)}, f32[2,1,130,1]{3,2,1,0:T(8,128)S(1)}, u32[]{:S(2)}, u32[]{:S(2)}) collective-permute-start(f32[2,1,130,1]{3,2,1,0:T(8,128)S(1)} %get-tuple-element.28), channel_id=1, source_target_pairs={{1,0},{2,1},{3,2},{5,4},{6,5},{7,6},{9,8},{10,9},{11,10},{13,12},{... | collective-permute-start | bytes 3128 | tf_op jit(solution)/shard_map/ppermute | solution.py:20
  188.7 4.0 collective-permute-start.19
  193.8 3.0 collective-permute-start.21
  195.4 5.5 %collective-permute-start.20 = (f32[2,1,1,1024]{3,2,1,0:T(1,128)S(1)}, f32[2,1,1,1024]{3,2,1,0:T(1,128)S(1)}, u32[]{:S(2)}, u32[]{:S(2)}) collective-permute-start(f32[2,1,1,1024]{3,2,1,0:T(1,128)S(1)} %get-tuple-element.47), channel_id=1, source_target_pairs={{4,0},{8,4},{12,8},{5,1},{9,5},{13,9},{6,2},{10,6},{14,10},{7,3},{... | collective-permute-start | bytes 24584 | tf_op jit(solution)/shard_map/ppermute | solution.py:20
  201.1 4.5 %collective-permute-start.22 = (f32[2,1,130,1]{3,2,1,0:T(8,128)S(1)}, f32[2,1,130,1]{3,2,1,0:T(8,128)S(1)}, u32[]{:S(2)}, u32[]{:S(2)}) collective-permute-start(f32[2,1,130,1]{3,2,1,0:T(8,128)S(1)} %get-tuple-element.26), channel_id=1, source_target_pairs={{1,0},{2,1},{3,2},{5,4},{6,5},{7,6},{9,8},{10,9},{11,10},{13,12},{... | collective-permute-start | bytes 3128 | tf_op jit(solution)/shard_map/ppermute | solution.py:20
  202.4 4.0 collective-permute-start.23
  211.5 3.3 collective-permute-start.25
  213.5 5.5 %collective-permute-start.24 = (f32[2,1,1,1024]{3,2,1,0:T(1,128)S(1)}, f32[2,1,1,1024]{3,2,1,0:T(1,128)S(1)}, u32[]{:S(2)}, u32[]{:S(2)}) collective-permute-start(f32[2,1,1,1024]{3,2,1,0:T(1,128)S(1)} %get-tuple-element.43), channel_id=1, source_target_pairs={{4,0},{8,4},{12,8},{5,1},{9,5},{13,9},{6,2},{10,6},{14,10},{7,3},{... | collective-permute-start | bytes 24584 | tf_op jit(solution)/shard_map/ppermute | solution.py:20
  219.1 6.5 %collective-permute-start.26 = (f32[2,1,130,1]{3,2,1,0:T(8,128)S(1)}, f32[2,1,130,1]{3,2,1,0:T(8,128)S(1)}, u32[]{:S(2)}, u32[]{:S(2)}) collective-permute-start(f32[2,1,130,1]{3,2,1,0:T(8,128)S(1)} %get-tuple-element.24), channel_id=1, source_target_pairs={{1,0},{2,1},{3,2},{5,4},{6,5},{7,6},{9,8},{10,9},{11,10},{13,12},{... | collective-permute-start | bytes 3128 | tf_op jit(solution)/shard_map/ppermute | solution.py:20
  220.4 6.2 %collective-permute-start.27 = (f32[2,1,130,1]{3,2,1,0:T(8,128)S(1)}, f32[2,1,130,1]{3,2,1,0:T(8,128)S(1)}, u32[]{:S(2)}, u32[]{:S(2)}) collective-permute-start(f32[2,1,130,1]{3,2,1,0:T(8,128)S(1)} %get-tuple-element.25), channel_id=1, source_target_pairs={{0,1},{1,2},{2,3},{4,5},{5,6},{6,7},{8,9},{9,10},{10,11},{12,13},{... | collective-permute-start | bytes 3128 | tf_op jit(solution)/shard_map/ppermute | solution.py:19
  227.9 3.6 collective-permute-start.29
  230.1 5.5 %collective-permute-start.28 = (f32[2,1,1,1024]{3,2,1,0:T(1,128)S(1)}, f32[2,1,1,1024]{3,2,1,0:T(1,128)S(1)}, u32[]{:S(2)}, u32[]{:S(2)}) collective-permute-start(f32[2,1,1,1024]{3,2,1,0:T(1,128)S(1)} %get-tuple-element.41), channel_id=1, source_target_pairs={{4,0},{8,4},{12,8},{5,1},{9,5},{13,9},{6,2},{10,6},{14,10},{7,3},{... | collective-permute-start | bytes 24584 | tf_op jit(solution)/shard_map/ppermute | solution.py:20
  235.8 7.1 %collective-permute-start.30 = (f32[2,1,130,1]{3,2,1,0:T(8,128)S(1)}, f32[2,1,130,1]{3,2,1,0:T(8,128)S(1)}, u32[]{:S(2)}, u32[]{:S(2)}) collective-permute-start(f32[2,1,130,1]{3,2,1,0:T(8,128)S(1)} %get-tuple-element.22), channel_id=1, source_target_pairs={{1,0},{2,1},{3,2},{5,4},{6,5},{7,6},{9,8},{10,9},{11,10},{13,12},{... | collective-permute-start | bytes 3128 | tf_op jit(solution)/shard_map/ppermute | solution.py:20
  237.1 6.7 %collective-permute-start.31 = (f32[2,1,130,1]{3,2,1,0:T(8,128)S(1)}, f32[2,1,130,1]{3,2,1,0:T(8,128)S(1)}, u32[]{:S(2)}, u32[]{:S(2)}) collective-permute-start(f32[2,1,130,1]{3,2,1,0:T(8,128)S(1)} %get-tuple-element.23), channel_id=1, source_target_pairs={{0,1},{1,2},{2,3},{4,5},{5,6},{6,7},{8,9},{9,10},{10,11},{12,13},{... | collective-permute-start | bytes 3128 | tf_op jit(solution)/shard_map/ppermute | solution.py:19
Sparse Core Ops, SparseCore 0:
  9.8 55.2 all-gather.1
  249.9 170.6 all-reduce.1
where the time goes:
time: 430 us; the launch traced here: 429 us
  waiting for transfers between devices  267 us (62%)
  starting transfers between devices  74.6 us (17%)
  other arithmetic  35.7 us (8%)
  blocking collectives  31.6 us (7%)
  between operations  14.8 us (3%)
  local copies, waits for them, and re-layouts  4.82 us (1%)
    psum x1, waiting for transfers between devices, per_device(): summed = lax.psum(local_grads, 'illum')  171 us
    all_gather x1, waiting for transfers between devices, per_device(): all_planes = lax.all_gather(phase_delay, 'illum', axis=1, tiled=True)  55.3 us
    ppermute x16, starting transfers between devices, with_halo(): before = lax.ppermute(last, axis, up)  53.8 us
    ppermute x16, waiting for transfers between devices, with_halo(): after = lax.ppermute(first, axis, down)  33.6 us
    psum x1, blocking collectives, per_device(): lax.psum(jnp.sum(target * target, axis=(0, 2, 3)), ('row', 'col'))  31.6 us
    ppermute x16, starting transfers between devices, with_halo(): after = lax.ppermute(first, axis, down)  20.8 us
  transfers between devices with their start and end apart: 34, of which 17 were waited for; matrix products, arithmetic and copies ran while one was open for 1% of the time, Pallas kernels for 0%

commit v1 on v0

--- a/solution.py
+++ b/solution.py
@@ -82,7 +82,8 @@
         / (total_rows * total_cols)
         + eps_energy
     )
-    all_planes = lax.all_gather(phase_delay, "illum", axis=1, tiled=True)
+    high = lax.all_to_all(jnp.stack(lax.axis_size("illum") * [phase_delay]), "illum", 0, 0)
+    all_planes = jnp.concatenate(high, axis=1)
     stored = []
     for depth_index in range(phase_delay.shape[0]):
         phase_plane = all_planes[depth_index]

time: 430 us -> 416 us (0.967)
  waiting for transfers between devices: 267 us -> 235 us
  starting transfers between devices: 74.6 us -> 87.6 us
    all_gather x1 -> x0, waiting for transfers between devices: 55.3 us -> none  [per_device(): all_planes = lax.all_gather(phase_delay, 'illum', axis=1, tiled=True)]
    all_to_all x0 -> x1, waiting for transfers between devices: none -> 24.2 us  [per_device(): lax.all_to_all(jnp.stack(lax.axis_size('illum') * [phase_delay]), 'illum'...]
    all_to_all x0 -> x1, starting transfers between devices: none -> 11.5 us  [per_device(): lax.all_to_all(jnp.stack(lax.axis_size('illum') * [phase_delay]), 'illum'...]
    sub x1 -> x2, other arithmetic: 4.14 us -> 12.8 us  [per_device(): adjoint_wave[1] * modulated[0] - adjoint_wave[0] * modulated[1]]
    another operation x9 -> x4, other arithmetic: 5.28 us -> 0.06 us  [propagate(): beside_all = neighbour_sum(exchange_rims(jnp.stack([real_part, imag_part])))]
    another operation x3 -> x2, other arithmetic: 4.85 us -> 0.03 us  [per_device(): jnp.stack([wave_field[0] * cosine - wave_field[1] * sine_part, wave_field...]
where the time goes in v1:
time: 416 us; the launch traced here: 415 us
  waiting for transfers between devices  235 us (56%)
  starting transfers between devices  87.6 us (21%)
  other arithmetic  39.8 us (10%)
  blocking collectives  31.6 us (8%)
  between operations  14.8 us (4%)
  local copies, waits for them, and re-layouts  6.33 us (2%)
    psum x1, waiting for transfers between devices, per_device(): summed = lax.psum(local_grads, 'illum')  170 us
    ppermute x16, starting transfers between devices, with_halo(): before = lax.ppermute(last, axis, up)  55.3 us
    ppermute x16, waiting for transfers between devices, with_halo(): after = lax.ppermute(first, axis, down)  33.6 us
    psum x1, blocking collectives, per_device(): lax.psum(jnp.sum(target * target, axis=(0, 2, 3)), ('row', 'col'))  31.6 us
    all_to_all x1, waiting for transfers between devices, per_device(): lax.all_to_all(jnp.stack(lax.axis_size('illum') * [phase_delay]), 'illum'...  24.2 us
    ppermute x16, starting transfers between devices, with_halo(): after = lax.ppermute(first, axis, down)  20.8 us
    sub x2, other arithmetic, per_device(): adjoint_wave[1] * modulated[0] - adjoint_wave[0] * modulated[1]  12.8 us
    all_to_all x1, starting transfers between devices, per_device(): lax.all_to_all(jnp.stack(lax.axis_size('illum') * [phase_delay]), 'illum'...  11.5 us
  transfers between devices with their start and end apart: 34, of which 17 were waited for; matrix products, arithmetic and copies ran while one was open for 1% of the time, Pallas kernels for 0%

profile of v1, /device:TPU:2, one launch (start us, length us, event | category | flops | bytes accessed | tf_op | source)
XLA Modules:
  0.0 414.9 jit_solution(8074191509832939042)
XLA Ops:
  6.5 2.0 stack.20
  8.5 11.5 %all-to-all-start = ((f32[16,2,8,1024]{3,2,1,0:T(8,128)}), f32[16,2,8,1024]{3,2,1,0:T(8,128)S(1)}, u32[]{:S(2)}, u32[]{:S(2)}) async-start(f32[16,2,8,1024]{3,2,1,0:T(8,128)} %stack.20), calls=%async_computation | async-start | bytes 2097152 | tf_op jit(solution)/shard_map/all_to_all | solution.py:85
  22.6 24.2 %all-to-all-done = f32[16,2,8,1024]{3,2,1,0:T(8,128)S(1)} async-done(((f32[16,2,8,1024]{3,2,1,0:T(8,128)}), f32[16,2,8,1024]{3,2,1,0:T(8,128)S(1)}, u32[]{:S(2)}, u32[]{:S(2)}) %all-to-all-start) | async-done | bytes 1048608 | tf_op jit(solution)/shard_map/all_to_all | solution.py:85
  46.7 3.8 fusion.47
  50.6 3.5 collective-permute-start.1
  54.1 1.3 collective-permute-start
  55.4 4.2 %collective-permute-done = f32[2,1,1,1024]{3,2,1,0:T(1,128)S(1)} collective-permute-done((f32[2,1,1,1024]{3,2,1,0:T(1,128)S(1)}, f32[2,1,1,1024]{3,2,1,0:T(1,128)S(1)}, u32[]{:S(2)}, u32[]{:S(2)}) %collective-permute-start) | collective-permute-done | bytes 8224 | tf_op jit(solution)/shard_map/ppermute | solution.py:20
  59.7 1.3 collective-permute-start.2
  61.0 3.0 collective-permute-start.3
  66.2 3.5 collective-permute-start.5
  69.7 1.3 collective-permute-start.4
  71.1 4.2 %collective-permute-done.4 = f32[2,1,1,1024]{3,2,1,0:T(1,128)S(1)} collective-permute-done((f32[2,1,1,1024]{3,2,1,0:T(1,128)S(1)}, f32[2,1,1,1024]{3,2,1,0:T(1,128)S(1)}, u32[]{:S(2)}, u32[]{:S(2)}) %collective-permute-start.4) | collective-permute-done | bytes 8224 | tf_op jit(solution)/shard_map/ppermute | solution.py:20
  75.4 1.3 collective-permute-start.6
  76.7 3.8 collective-permute-start.7
  82.1 2.1 fusion.44
  84.3 2.0 fusion.43
  86.3 3.2 collective-permute-start.9
  89.5 1.3 collective-permute-start.8
  90.8 4.2 %collective-permute-done.8 = f32[2,1,1,1024]{3,2,1,0:T(1,128)S(1)} collective-permute-done((f32[2,1,1,1024]{3,2,1,0:T(1,128)S(1)}, f32[2,1,1,1024]{3,2,1,0:T(1,128)S(1)}, u32[]{:S(2)}, u32[]{:S(2)}) %collective-permute-start.8) | collective-permute-done | bytes 8224 | tf_op jit(solution)/shard_map/ppermute | solution.py:20
  95.1 1.3 collective-permute-start.10
  96.4 6.0 %collective-permute-start.11 = (f32[2,1,130,1]{3,2,1,0:T(8,128)S(1)}, f32[2,1,130,1]{3,2,1,0:T(8,128)S(1)}, u32[]{:S(2)}, u32[]{:S(2)}) collective-permute-start(f32[2,1,130,1]{3,2,1,0:T(8,128)S(1)} %get-tuple-element.38), channel_id=1, source_target_pairs={{0,1},{1,2},{2,3},{4,5},{5,6},{6,7},{8,9},{9,10},{10,11},{12,13},{... | collective-permute-start | bytes 3128 | tf_op jit(solution)/shard_map/ppermute | solution.py:19
  105.4 2.2 collective-permute-start.13
  107.6 1.4 collective-permute-start.12
  109.1 4.2 %collective-permute-done.12 = f32[2,1,1,1024]{3,2,1,0:T(1,128)S(1)} collective-permute-done((f32[2,1,1,1024]{3,2,1,0:T(1,128)S(1)}, f32[2,1,1,1024]{3,2,1,0:T(1,128)S(1)}, u32[]{:S(2)}, u32[]{:S(2)}) %collective-permute-start.12) | collective-permute-done | bytes 8224 | tf_op jit(solution)/shard_map/ppermute | solution.py:20
  115.4 5.7 %collective-permute-start.15 = (f32[2,1,130,1]{3,2,1,0:T(8,128)}, f32[2,1,130,1]{3,2,1,0:T(8,128)S(1)}, u32[]{:S(2)}, u32[]{:S(2)}) collective-permute-start(f32[2,1,130,1]{3,2,1,0:T(8,128)} %get-tuple-element.36), channel_id=1, source_target_pairs={{0,1},{1,2},{2,3},{4,5},{5,6},{6,7},{8,9},{9,10},{10,11},{12,13},{... | collective-permute-start | bytes 3128 | tf_op jit(solution)/shard_map/ppermute | solution.py:19
  122.0 31.6 %psum.14 = f32[1]{0:T(128)} all-reduce(f32[1]{0:T(128)} %bitcast.7), channel_id=1, replica_groups=mesh['illum'=16,'row'=4,'col'=4] {'row','col'}, use_global_device_ids=true, to_apply=%region_1.2 | all-reduce | flops 1 | bytes 8 | tf_op jit(solution)/shard_map/psum | solution.py:81
  154.3 3.2 fusion.15
  160.1 1.3 collective-permute-start.16
  161.4 4.2 %collective-permute-done.16 = f32[2,1,1,1024]{3,2,1,0:T(1,128)S(1)} collective-permute-done((f32[2,1,1,1024]{3,2,1,0:T(1,128)S(1)}, f32[2,1,1,1024]{3,2,1,0:T(1,128)S(1)}, u32[]{:S(2)}, u32[]{:S(2)}) %collective-permute-start.16) | collective-permute-done | bytes 8224 | tf_op jit(solution)/shard_map/ppermute | solution.py:20
  165.8 1.3 collective-permute-start.18
  167.1 3.0 collective-permute-start.19
  172.4 1.6 collective-permute-start.21
  174.0 1.3 collective-permute-start.20
  175.4 4.2 %collective-permute-done.20 = f32[2,1,1,1024]{3,2,1,0:T(1,128)S(1)} collective-permute-done((f32[2,1,1,1024]{3,2,1,0:T(1,128)S(1)}, f32[2,1,1,1024]{3,2,1,0:T(1,128)S(1)}, u32[]{:S(2)}, u32[]{:S(2)}) %collective-permute-start.20) | collective-permute-done | bytes 8224 | tf_op jit(solution)/shard_map/ppermute | solution.py:20
  179.7 1.3 collective-permute-start.22
  181.0 3.2 collective-permute-start.23
  185.7 2.1 fusion.45
  187.8 2.0 fusion.46
  189.8 1.9 collective-permute-start.25
  193.1 4.2 %collective-permute-done.24 = f32[2,1,1,1024]{3,2,1,0:T(1,128)S(1)} collective-permute-done((f32[2,1,1,1024]{3,2,1,0:T(1,128)S(1)}, f32[2,1,1,1024]{3,2,1,0:T(1,128)S(1)}, u32[]{:S(2)}, u32[]{:S(2)}) %collective-permute-start.24) | collective-permute-done | bytes 8224 | tf_op jit(solution)/shard_map/ppermute | solution.py:20
  198.7 5.2 %collective-permute-start.27 = (f32[2,1,130,1]{3,2,1,0:T(8,128)S(1)}, f32[2,1,130,1]{3,2,1,0:T(8,128)S(1)}, u32[]{:S(2)}, u32[]{:S(2)}) collective-permute-start(f32[2,1,130,1]{3,2,1,0:T(8,128)S(1)} %get-tuple-element.30), channel_id=1, source_target_pairs={{0,1},{1,2},{2,3},{4,5},{5,6},{6,7},{8,9},{9,10},{10,11},{12,13},{... | collective-permute-start | bytes 3128 | tf_op jit(solution)/shard_map/ppermute | solution.py:19
  206.0 2.2 collective-permute-start.29
  209.5 4.2 %collective-permute-done.28 = f32[2,1,1,1024]{3,2,1,0:T(1,128)S(1)} collective-permute-done((f32[2,1,1,1024]{3,2,1,0:T(1,128)S(1)}, f32[2,1,1,1024]{3,2,1,0:T(1,128)S(1)}, u32[]{:S(2)}, u32[]{:S(2)}) %collective-permute-start.28) | collective-permute-done | bytes 8224 | tf_op jit(solution)/shard_map/ppermute | solution.py:20
  215.1 5.7 %collective-permute-start.31 = (f32[2,1,130,1]{3,2,1,0:T(8,128)S(1)}, f32[2,1,130,1]{3,2,1,0:T(8,128)S(1)}, u32[]{:S(2)}, u32[]{:S(2)}) collective-permute-start(f32[2,1,130,1]{3,2,1,0:T(8,128)S(1)} %get-tuple-element.28), channel_id=1, source_target_pairs={{0,1},{1,2},{2,3},{4,5},{5,6},{6,7},{8,9},{9,10},{10,11},{12,13},{... | collective-permute-start | bytes 3128 | tf_op jit(solution)/shard_map/ppermute | solution.py:19
  222.6 6.5 %multiply_subtract_fusion = (f32[1,128,1024]{2,1,0:T(8,128)S(1)}, f32[1,128,1024]{2,1,0:T(8,128)S(1)}, f32[1,128,1024]{2,1,0:T(8,128)S(1)}) fusion(f32[2,1,128,1024]{3,2,1,0:T(8,128)S(1)} %fusion.3, f32[2,1,128,1024]{3,2,1,0:T(8,128)S(1)} %fusion.6, f32[2,16,8,1024]{3,2,0,1:T(8,128)S(1)} %bitcast.200, f32[1024]{0:T(1024)S(1)} %fusion.65, ...), kind=kLoop, calls=%fused_computation.199 | loop fusion | flops 6946816 | bytes 7868928 | tf_op jit(solution)/shard_map/sub | solution.py:106
  229.1 6.3 %fusion.39 = f32[1,128,1024]{2,1,0:T(8,128)S(1)} fusion(f32[2,1,128,1024]{3,2,1,0:T(8,128)S(1)} %fusion.21, f32[2,1,128,1024]{3,2,1,0:T(8,128)S(1)} %fusion.24, f32[2,16,8,1024]{3,2,0,1:T(8,128)S(1)} %bitcast.201, f32[1,128,1024]{2,1,0:T(8,128)S(1)} %get-tuple-element.7, f32[1,128,1024]{2,1,0:T(8,128)S(1)} %get-tuple-element.6, f32[1024]{0:T(1024)S(1)} %fusion.65, ...), kind=kLoop, calls=%fused_computation.166 | loop fusion | flops 5373952 | bytes 4723200 | tf_op jit(solution)/shard_map/sub | solution.py:106
  236.4 170.1 %all-reduce.2.cloned.1.call-done = f32[2,128,1024]{2,1,0:T(8,128)} async-done(((f32[2,128,1024]{2,1,0:T(8,128)}), f32[2,128,1024]{2,1,0:T(8,128)}) %all-reduce.2.cloned.1.call-update) | async-done | bytes 1048592 | tf_op jit(solution)/shard_map/psum | solution.py:116
  406.5 1.5 constant_dynamic-slice_fusion
  (87 shorter events, 29.4 us)
Async XLA Ops:
  8.5 38.2 %all-to-all-start = ((f32[16,2,8,1024]{3,2,1,0:T(8,128)}), f32[16,2,8,1024]{3,2,1,0:T(8,128)S(1)}, u32[]{:S(2)}, u32[]{:S(2)}) async-start(f32[16,2,8,1024]{3,2,1,0:T(8,128)} %stack.20), calls=%async_computation | async-start | bytes 2097152 | tf_op jit(solution)/shard_map/all_to_all | solution.py:85
  20.0 386.5 %all-reduce.2.cloned.1.call-start = ((), (), s32[]{:S(2)}) async-start(), calls=%async_computation.1 | async-start | bytes 2097152 | tf_op jit(solution)/shard_map/psum | solution.py:116
  20.0 0.7 copy-start.8
  50.6 4.8 %collective-permute-start.1 = (f32[2,1,1,1024]{3,2,1,0:T(1,128)S(1)}, f32[2,1,1,1024]{3,2,1,0:T(1,128)S(1)}, u32[]{:S(2)}, u32[]{:S(2)}) collective-permute-start(f32[2,1,1,1024]{3,2,1,0:T(1,128)S(1)} %get-tuple-element.59), channel_id=1, source_target_pairs={{0,4},{4,8},{8,12},{1,5},{5,9},{9,13},{2,6},{6,10},{10,14},{3,7},{... | collective-permute-start | bytes 24584 | tf_op jit(solution)/shard_map/ppermute | solution.py:19
  54.1 5.5 %collective-permute-start = (f32[2,1,1,1024]{3,2,1,0:T(1,128)S(1)}, f32[2,1,1,1024]{3,2,1,0:T(1,128)S(1)}, u32[]{:S(2)}, u32[]{:S(2)}) collective-permute-start(f32[2,1,1,1024]{3,2,1,0:T(1,128)S(1)} %get-tuple-element.60), channel_id=1, source_target_pairs={{4,0},{8,4},{12,8},{5,1},{9,5},{13,9},{6,2},{10,6},{14,10},{7,3},{... | collective-permute-start | bytes 24584 | tf_op jit(solution)/shard_map/ppermute | solution.py:20
  59.7 4.3 %collective-permute-start.2 = (f32[2,1,130,1]{3,2,1,0:T(8,128)S(1)}, f32[2,1,130,1]{3,2,1,0:T(8,128)S(1)}, u32[]{:S(2)}, u32[]{:S(2)}) collective-permute-start(f32[2,1,130,1]{3,2,1,0:T(8,128)S(1)} %get-tuple-element.41), channel_id=1, source_target_pairs={{1,0},{2,1},{3,2},{5,4},{6,5},{7,6},{9,8},{10,9},{11,10},{13,12},{... | collective-permute-start | bytes 3128 | tf_op jit(solution)/shard_map/ppermute | solution.py:20
  61.0 4.0 collective-permute-start.3
  66.2 4.8 %collective-permute-start.5 = (f32[2,1,1,1024]{3,2,1,0:T(1,128)S(1)}, f32[2,1,1,1024]{3,2,1,0:T(1,128)S(1)}, u32[]{:S(2)}, u32[]{:S(2)}) collective-permute-start(f32[2,1,1,1024]{3,2,1,0:T(1,128)S(1)} %get-tuple-element.57), channel_id=1, source_target_pairs={{0,4},{4,8},{8,12},{1,5},{5,9},{9,13},{2,6},{6,10},{10,14},{3,7},{... | collective-permute-start | bytes 24584 | tf_op jit(solution)/shard_map/ppermute | solution.py:19
  69.7 5.5 %collective-permute-start.4 = (f32[2,1,1,1024]{3,2,1,0:T(1,128)S(1)}, f32[2,1,1,1024]{3,2,1,0:T(1,128)S(1)}, u32[]{:S(2)}, u32[]{:S(2)}) collective-permute-start(f32[2,1,1,1024]{3,2,1,0:T(1,128)S(1)} %get-tuple-element.58), channel_id=1, source_target_pairs={{4,0},{8,4},{12,8},{5,1},{9,5},{13,9},{6,2},{10,6},{14,10},{7,3},{... | collective-permute-start | bytes 24584 | tf_op jit(solution)/shard_map/ppermute | solution.py:20
  75.4 5.1 %collective-permute-start.6 = (f32[2,1,130,1]{3,2,1,0:T(8,128)S(1)}, f32[2,1,130,1]{3,2,1,0:T(8,128)S(1)}, u32[]{:S(2)}, u32[]{:S(2)}) collective-permute-start(f32[2,1,130,1]{3,2,1,0:T(8,128)S(1)} %get-tuple-element.39), channel_id=1, source_target_pairs={{1,0},{2,1},{3,2},{5,4},{6,5},{7,6},{9,8},{10,9},{11,10},{13,12},{... | collective-permute-start | bytes 3128 | tf_op jit(solution)/shard_map/ppermute | solution.py:20
  76.7 4.8 %collective-permute-start.7 = (f32[2,1,130,1]{3,2,1,0:T(8,128)S(1)}, f32[2,1,130,1]{3,2,1,0:T(8,128)S(1)}, u32[]{:S(2)}, u32[]{:S(2)}) collective-permute-start(f32[2,1,130,1]{3,2,1,0:T(8,128)S(1)} %get-tuple-element.40), channel_id=1, source_target_pairs={{0,1},{1,2},{2,3},{4,5},{5,6},{6,7},{8,9},{9,10},{10,11},{12,13},{... | collective-permute-start | bytes 3128 | tf_op jit(solution)/shard_map/ppermute | solution.py:19
  86.3 4.5 %collective-permute-start.9 = (f32[2,1,1,1024]{3,2,1,0:T(1,128)S(1)}, f32[2,1,1,1024]{3,2,1,0:T(1,128)S(1)}, u32[]{:S(2)}, u32[]{:S(2)}) collective-permute-start(f32[2,1,1,1024]{3,2,1,0:T(1,128)S(1)} %get-tuple-element.55), channel_id=1, source_target_pairs={{0,4},{4,8},{8,12},{1,5},{5,9},{9,13},{2,6},{6,10},{10,14},{3,7},{... | collective-permute-start | bytes 24584 | tf_op jit(solution)/shard_map/ppermute | solution.py:19
  89.5 5.5 %collective-permute-start.8 = (f32[2,1,1,1024]{3,2,1,0:T(1,128)S(1)}, f32[2,1,1,1024]{3,2,1,0:T(1,128)S(1)}, u32[]{:S(2)}, u32[]{:S(2)}) collective-permute-start(f32[2,1,1,1024]{3,2,1,0:T(1,128)S(1)} %get-tuple-element.56), channel_id=1, source_target_pairs={{4,0},{8,4},{12,8},{5,1},{9,5},{13,9},{6,2},{10,6},{14,10},{7,3},{... | collective-permute-start | bytes 24584 | tf_op jit(solution)/shard_map/ppermute | solution.py:20
  95.1 7.3 %collective-permute-start.10 = (f32[2,1,130,1]{3,2,1,0:T(8,128)S(1)}, f32[2,1,130,1]{3,2,1,0:T(8,128)S(1)}, u32[]{:S(2)}, u32[]{:S(2)}) collective-permute-start(f32[2,1,130,1]{3,2,1,0:T(8,128)S(1)} %get-tuple-element.37), channel_id=1, source_target_pairs={{1,0},{2,1},{3,2},{5,4},{6,5},{7,6},{9,8},{10,9},{11,10},{13,12},{... | collective-permute-start | bytes 3128 | tf_op jit(solution)/shard_map/ppermute | solution.py:20
  96.4 7.0 %collective-permute-start.11 = (f32[2,1,130,1]{3,2,1,0:T(8,128)S(1)}, f32[2,1,130,1]{3,2,1,0:T(8,128)S(1)}, u32[]{:S(2)}, u32[]{:S(2)}) collective-permute-start(f32[2,1,130,1]{3,2,1,0:T(8,128)S(1)} %get-tuple-element.38), channel_id=1, source_target_pairs={{0,1},{1,2},{2,3},{4,5},{5,6},{6,7},{8,9},{9,10},{10,11},{12,13},{... | collective-permute-start | bytes 3128 | tf_op jit(solution)/shard_map/ppermute | solution.py:19
  104.4 0.8 copy-start.2
  104.4 1.0 copy-start.4
  104.4 8.9 %copy-start = (f32[1,1,128,1024]{3,2,1,0:T(8,128)}, f32[1,1,128,1024]{3,2,1,0:T(8,128)S(1)}, u32[]{:S(2)}) copy-start(f32[1,1,128,1024]{3,2,1,0:T(8,128)S(1)} %get-tuple-element.14) | copy-start | bytes 1572868
  105.4 7.9 %copy-start.1 = (f32[1,1,128,1024]{3,2,1,0:T(8,128)}, f32[1,1,128,1024]{3,2,1,0:T(8,128)S(1)}, u32[]{:S(2)}) copy-start(f32[1,1,128,1024]{3,2,1,0:T(8,128)S(1)} %subtract_multiply_fusion.5) | copy-start | bytes 1572868
  105.4 3.7 collective-permute-start.13
  107.6 13.5 %copy-start.6 = (bf16[2,1,128,1024]{3,2,1,0:T(8,128)(2,1)S(1)}, bf16[2,1,128,1024]{3,2,1,0:T(8,128)(2,1)}, u32[]{:S(2)}) copy-start(bf16[2,1,128,1024]{3,2,1,0:T(8,128)(2,1)} %param.5) | copy-start | bytes 1572868
  107.6 5.7 %collective-permute-start.12 = (f32[2,1,1,1024]{3,2,1,0:T(1,128)S(1)}, f32[2,1,1,1024]{3,2,1,0:T(1,128)S(1)}, u32[]{:S(2)}, u32[]{:S(2)}) collective-permute-start(f32[2,1,1,1024]{3,2,1,0:T(1,128)S(1)} %get-tuple-element.54), channel_id=1, source_target_pairs={{4,0},{8,4},{12,8},{5,1},{9,5},{13,9},{6,2},{10,6},{14,10},{7,3},{... | collective-permute-start | bytes 24584 | tf_op jit(solution)/shard_map/ppermute | solution.py:20
  114.1 40.2 %collective-permute-start.14 = (f32[2,1,130,1]{3,2,1,0:T(8,128)}, f32[2,1,130,1]{3,2,1,0:T(8,128)S(1)}, u32[]{:S(2)}, u32[]{:S(2)}) collective-permute-start(f32[2,1,130,1]{3,2,1,0:T(8,128)} %get-tuple-element.35), channel_id=1, source_target_pairs={{1,0},{2,1},{3,2},{5,4},{6,5},{7,6},{9,8},{10,9},{11,10},{13,12},{... | collective-permute-start | bytes 3128 | tf_op jit(solution)/shard_map/ppermute | solution.py:20
  115.4 38.9 %collective-permute-start.15 = (f32[2,1,130,1]{3,2,1,0:T(8,128)}, f32[2,1,130,1]{3,2,1,0:T(8,128)S(1)}, u32[]{:S(2)}, u32[]{:S(2)}) collective-permute-start(f32[2,1,130,1]{3,2,1,0:T(8,128)} %get-tuple-element.36), channel_id=1, source_target_pairs={{0,1},{1,2},{2,3},{4,5},{5,6},{6,7},{8,9},{9,10},{10,11},{12,13},{... | collective-permute-start | bytes 3128 | tf_op jit(solution)/shard_map/ppermute | solution.py:19
  154.3 3.2 copy-start.3
  154.3 3.2 copy-start.5
  157.6 1.0 copy-start.7
  158.8 2.6 collective-permute-start.17
  160.1 5.5 %collective-permute-start.16 = (f32[2,1,1,1024]{3,2,1,0:T(1,128)S(1)}, f32[2,1,1,1024]{3,2,1,0:T(1,128)S(1)}, u32[]{:S(2)}, u32[]{:S(2)}) collective-permute-start(f32[2,1,1,1024]{3,2,1,0:T(1,128)S(1)} %get-tuple-element.52), channel_id=1, source_target_pairs={{4,0},{8,4},{12,8},{5,1},{9,5},{13,9},{6,2},{10,6},{14,10},{7,3},{... | collective-permute-start | bytes 24584 | tf_op jit(solution)/shard_map/ppermute | solution.py:20
  165.8 4.3 %collective-permute-start.18 = (f32[2,1,130,1]{3,2,1,0:T(8,128)S(1)}, f32[2,1,130,1]{3,2,1,0:T(8,128)S(1)}, u32[]{:S(2)}, u32[]{:S(2)}) collective-permute-start(f32[2,1,130,1]{3,2,1,0:T(8,128)S(1)} %get-tuple-element.33), channel_id=1, source_target_pairs={{1,0},{2,1},{3,2},{5,4},{6,5},{7,6},{9,8},{10,9},{11,10},{13,12},{... | collective-permute-start | bytes 3128 | tf_op jit(solution)/shard_map/ppermute | solution.py:20
  167.1 4.0 collective-permute-start.19
  172.4 3.0 collective-permute-start.21
  174.0 5.5 %collective-permute-start.20 = (f32[2,1,1,1024]{3,2,1,0:T(1,128)S(1)}, f32[2,1,1,1024]{3,2,1,0:T(1,128)S(1)}, u32[]{:S(2)}, u32[]{:S(2)}) collective-permute-start(f32[2,1,1,1024]{3,2,1,0:T(1,128)S(1)} %get-tuple-element.50), channel_id=1, source_target_pairs={{4,0},{8,4},{12,8},{5,1},{9,5},{13,9},{6,2},{10,6},{14,10},{7,3},{... | collective-permute-start | bytes 24584 | tf_op jit(solution)/shard_map/ppermute | solution.py:20
  179.7 4.5 %collective-permute-start.22 = (f32[2,1,130,1]{3,2,1,0:T(8,128)S(1)}, f32[2,1,130,1]{3,2,1,0:T(8,128)S(1)}, u32[]{:S(2)}, u32[]{:S(2)}) collective-permute-start(f32[2,1,130,1]{3,2,1,0:T(8,128)S(1)} %get-tuple-element.31), channel_id=1, source_target_pairs={{1,0},{2,1},{3,2},{5,4},{6,5},{7,6},{9,8},{10,9},{11,10},{13,12},{... | collective-permute-start | bytes 3128 | tf_op jit(solution)/shard_map/ppermute | solution.py:20
  181.0 4.0 collective-permute-start.23
  189.8 3.3 collective-permute-start.25
  191.8 5.5 %collective-permute-start.24 = (f32[2,1,1,1024]{3,2,1,0:T(1,128)S(1)}, f32[2,1,1,1024]{3,2,1,0:T(1,128)S(1)}, u32[]{:S(2)}, u32[]{:S(2)}) collective-permute-start(f32[2,1,1,1024]{3,2,1,0:T(1,128)S(1)} %get-tuple-element.48), channel_id=1, source_target_pairs={{4,0},{8,4},{12,8},{5,1},{9,5},{13,9},{6,2},{10,6},{14,10},{7,3},{... | collective-permute-start | bytes 24584 | tf_op jit(solution)/shard_map/ppermute | solution.py:20
  197.4 6.5 %collective-permute-start.26 = (f32[2,1,130,1]{3,2,1,0:T(8,128)S(1)}, f32[2,1,130,1]{3,2,1,0:T(8,128)S(1)}, u32[]{:S(2)}, u32[]{:S(2)}) collective-permute-start(f32[2,1,130,1]{3,2,1,0:T(8,128)S(1)} %get-tuple-element.29), channel_id=1, source_target_pairs={{1,0},{2,1},{3,2},{5,4},{6,5},{7,6},{9,8},{10,9},{11,10},{13,12},{... | collective-permute-start | bytes 3128 | tf_op jit(solution)/shard_map/ppermute | solution.py:20
  198.7 6.2 %collective-permute-start.27 = (f32[2,1,130,1]{3,2,1,0:T(8,128)S(1)}, f32[2,1,130,1]{3,2,1,0:T(8,128)S(1)}, u32[]{:S(2)}, u32[]{:S(2)}) collective-permute-start(f32[2,1,130,1]{3,2,1,0:T(8,128)S(1)} %get-tuple-element.30), channel_id=1, source_target_pairs={{0,1},{1,2},{2,3},{4,5},{5,6},{6,7},{8,9},{9,10},{10,11},{12,13},{... | collective-permute-start | bytes 3128 | tf_op jit(solution)/shard_map/ppermute | solution.py:19
  206.0 3.6 collective-permute-start.29
  208.2 5.5 %collective-permute-start.28 = (f32[2,1,1,1024]{3,2,1,0:T(1,128)S(1)}, f32[2,1,1,1024]{3,2,1,0:T(1,128)S(1)}, u32[]{:S(2)}, u32[]{:S(2)}) collective-permute-start(f32[2,1,1,1024]{3,2,1,0:T(1,128)S(1)} %get-tuple-element.46), channel_id=1, source_target_pairs={{4,0},{8,4},{12,8},{5,1},{9,5},{13,9},{6,2},{10,6},{14,10},{7,3},{... | collective-permute-start | bytes 24584 | tf_op jit(solution)/shard_map/ppermute | solution.py:20
  213.8 7.1 %collective-permute-start.30 = (f32[2,1,130,1]{3,2,1,0:T(8,128)S(1)}, f32[2,1,130,1]{3,2,1,0:T(8,128)S(1)}, u32[]{:S(2)}, u32[]{:S(2)}) collective-permute-start(f32[2,1,130,1]{3,2,1,0:T(8,128)S(1)} %get-tuple-element.27), channel_id=1, source_target_pairs={{1,0},{2,1},{3,2},{5,4},{6,5},{7,6},{9,8},{10,9},{11,10},{13,12},{... | collective-permute-start | bytes 3128 | tf_op jit(solution)/shard_map/ppermute | solution.py:20
  215.1 6.7 %collective-permute-start.31 = (f32[2,1,130,1]{3,2,1,0:T(8,128)S(1)}, f32[2,1,130,1]{3,2,1,0:T(8,128)S(1)}, u32[]{:S(2)}, u32[]{:S(2)}) collective-permute-start(f32[2,1,130,1]{3,2,1,0:T(8,128)S(1)} %get-tuple-element.28), channel_id=1, source_target_pairs={{0,1},{1,2},{2,3},{4,5},{5,6},{6,7},{8,9},{9,10},{10,11},{12,13},{... | collective-permute-start | bytes 3128 | tf_op jit(solution)/shard_map/ppermute | solution.py:19
Sparse Core Ops, SparseCore 0:
  236.6 169.9 all-reduce.1
